TPU v7x, 32 devices: a whole 2x2x4 slice. The times are simulated.
32 devices in a mesh: row: 4 (over y, x), col: 8 (over z, core).
Axes of the slice: x: 2, y: 2, z: 4, core: 2. Of those that a mesh axis runs over, the one named last changes fastest.
Arguments:
- xblocks: bfloat16 [56, 8, 128, 128], P('row', 'col'), may hold values from -2 to 2
- xcols: int32 [56, 8], P('row', 'col'), may hold values from 0 to 6, as said below
- outcols: int32 [56, 16], P('row', 'col'), may hold values from 0 to 6, as said below
Outputs:
- square_blocks: bfloat16 [56, 16, 128, 128], P('row', 'col')
Inputs may be any that keep to these rules, and one draw needn't show every extreme that they name: xcols[m, t] is a block column within column tile t; over all block rows, the entries of one column tile take at most 3 distinct values. `outcols`: each entry names a block column of its column tile at which at least one block product of the window for that block row lands; entries of one row and tile may repeat.
All inputs are finite; a program needn't handle non-finite values.
Results may differ from a plain program's by a relative error of at most 0.001.
Values may be sent and summed in bfloat16 or wider, within the bound.
A program may use at most 64 MiB of HBM per device.

v0:
```python
import jax
import jax.numpy as jnp
from jax import lax
from jax.sharding import PartitionSpec as P

STEPS = 4


def passed_along(value, axis, steps):
    count = lax.axis_size(axis)
    pairs = [(source, (source + steps) % count) for source in range(count)]
    return lax.ppermute(value, axis, pairs)


def broadcast(value, axis, source):
    kept = jnp.where(lax.axis_index(axis) == source, value, 0).astype(value.dtype)
    return lax.psum(kept, axis)


def add_products(total, a_blocks, a_cols, b_blocks, b_cols, targets, offset):
    index = offset + a_cols
    chosen = jnp.take(b_blocks, index, axis=0)
    landing = jnp.take(b_cols, index, axis=0)
    product = jnp.einsum("mab,mbc->mac", a_blocks, chosen, preferred_element_type=jnp.float32)
    weight = (landing[:, None] == targets).astype(jnp.float32)
    return total + weight[:, :, None, None] * product[:, None]


def on_device(xblocks, xcols, outcols):
    row_count = lax.axis_size("row")
    col_count = lax.axis_size("col")
    per_panel = col_count // row_count
    block_rows = xblocks.shape[0]
    tile_cols = block_rows // per_panel
    block_size = xblocks.shape[2]
    kept = outcols.shape[1]
    row_here = lax.axis_index("row")
    own_blocks = xblocks[:, 0]
    own_cols = xcols[:, 0]
    total = jnp.zeros((block_rows, kept, block_size, block_size), jnp.float32)
    moving = (own_blocks, own_cols)
    for step_no in range(STEPS):
        panel = (row_here + step_no) % row_count
        if step_no > 0:
            moving = passed_along((moving[0], moving[1]), "row", -1)
        for half_no in range(per_panel):
            tile_blocks, tile_cols_ids = (
                broadcast(own_blocks, "col", per_panel * panel + half_no),
                broadcast(own_cols, "col", per_panel * panel + half_no),
            )
            total = add_products(
                total,
                tile_blocks,
                tile_cols_ids,
                moving[0],
                moving[1],
                outcols,
                half_no * tile_cols,
            )
    return total.astype(jnp.bfloat16)


def solution(mesh):
    in_specs = (P("row", "col", None, None), P("row", "col"), P("row", "col"))
    out_specs = P("row", "col", None, None)
    return jax.shard_map(
        on_device, mesh=mesh, in_specs=in_specs, out_specs=out_specs, check_vma=False
    )
```

profile of v0, /device:TPU:1, one launch (start us, length us, event | category | flops | bytes accessed | tf_op | source)
XLA Modules:
  0.0 119.8 jit_solution(17391470564263204695)
XLA Ops:
  6.5 0.0 all-reduce.4.cloned.1.call-start
  6.5 3.0 %collective-permute-start.1 = (bf16[14,128,128]{2,1,0:T(8,128)(2,1)}, bf16[14,128,128]{2,1,0:T(8,128)(2,1)S(1)}, u32[]{:S(2)}, u32[]{:S(2)}) collective-permute-start(bf16[14,128,128]{2,1,0:T(8,128)(2,1)} %bitcast.29), channel_id=1, source_target_pairs={{0,24},{8,0},{16,8},{24,16},{1,25},{9,1},{17,9},{25,17},{2,26},{10... | collective-permute-start | bytes 1376264 | tf_op jit(solution)/shard_map/ppermute | solution.py:12
  9.5 0.3 collective-permute-start
  9.8 2.9 %broadcast_select_fusion.7 = (bf16[14,128,128]{2,1,0:T(8,128)(2,1)}, bf16[14,128,128]{2,1,0:T(8,128)(2,1)}, bf16[14,128,128]{2,1,0:T(8,128)(2,1)}, bf16[14,128,1...) fusion(pred[]{:T(512)S(6)} %eq.101, ...), kind=kLoop, calls=%fused_computation.48 | loop fusion | flops 1835008 | bytes 4128776 | tf_op jit(solution)/shard_map/jit(_where)/select_n | solution.py:16
  12.7 0.0 copy-start
  12.7 0.0 all-reduce.4.cloned.1.call-update
  12.7 0.6 copy-done
  13.4 8.7 %all-reduce = (s32[14]{0:T(128)S(1)}, s32[14]{0:T(128)S(1)}, s32[14]{0:T(128)S(1)}, s32[14]{0:T(128)S(1)}, s32[14]{0:T(128)S(1)}, /*index=5*/s32[14]{0:T(128)S(1)}, s32[14]{0:T(128)S(1)}, s32[14]{0:T(128)S(1)}) all-reduce(s32[14]{0:T(128)S(1)} %get-tuple-element.62, ...), channel_id=1, replica_groups=mesh['row'=4,'col'=8] {'col'}, use_global_device_ids=true, to_apply=%region_14.17 | all-reduce | flops 112 | bytes 896 | tf_op jit(solution)/shard_map/psum | solution.py:17
  22.3 0.7 gather_fusion.2
  23.0 0.0 copy-done.1
  23.0 0.6 gather_fusion.3
  23.6 0.7 gather_fusion
  24.3 0.6 gather_fusion.1
  24.9 0.0 collective-permute-done
  25.0 1.2 collective-permute-start.2
  26.1 0.7 gather_fusion.6
  26.8 0.7 gather_fusion.4
  27.5 0.0 collective-permute-done.1
  27.5 0.2 collective-permute-start.3
  27.7 0.1 collective-permute-done.2
  27.8 2.2 %collective-permute-start.4 = (s32[14]{0:T(128)S(1)}, s32[14]{0:T(128)S(1)}, u32[]{:S(2)}, u32[]{:S(2)}) collective-permute-start(s32[14]{0:T(128)S(1)} %collective-permute-done.2), channel_id=1, source_target_pairs={{0,24},{8,0},{16,8},{24,16},{1,25},{9,1},{17,9},{25,17},{2,26},{10... | collective-permute-start | bytes 176 | tf_op jit(solution)/shard_map/ppermute | solution.py:12
  30.0 0.7 gather_fusion.10
  30.7 0.7 gather_fusion.8
  31.3 6.0 %collective-permute-done.4 = s32[14]{0:T(128)S(1)} collective-permute-done((s32[14]{0:T(128)S(1)}, s32[14]{0:T(128)S(1)}, u32[]{:S(2)}, u32[]{:S(2)}) %collective-permute-start.4) | collective-permute-done | bytes 88 | tf_op jit(solution)/shard_map/ppermute | solution.py:12
  37.4 0.7 gather_fusion.14
  38.0 0.0 collective-permute-done.3
  38.0 1.0 collective-permute-start.5
  39.0 0.7 gather_fusion.12
  39.7 0.0 copy-done.10
  39.7 0.1 copy.19
  39.8 0.1 copy.18
  39.9 0.1 copy.17
  40.0 0.1 copy.16
  40.1 0.1 copy.15
  40.2 0.1 copy.14
  40.3 0.1 copy.13
  40.4 0.1 copy.12
  40.5 0.6 gather_fusion.7
  41.1 0.6 gather_fusion.5
  41.8 1.4 %gather_fusion.11 = bf16[14,128,128]{2,1,0:T(8,128)(2,1)} fusion(bf16[14,128,128]{2,1,0:T(8,128)(2,1)S(1)} %collective-permute-done.3, s32[1024]{0:T(1024)S(1)} %pad_clamp_fusion.2), kind=kCustom, calls=%fused_computation.13.clone | custom fusion | bytes 917560 | tf_op jit(solution)/shard_map/jit(_take)/gather | solution.py:22
  43.2 0.6 gather_fusion.9
  43.8 3.2 %collective-permute-done.5 = bf16[14,128,128]{2,1,0:T(8,128)(2,1)S(1)} collective-permute-done((bf16[14,128,128]{2,1,0:T(8,128)(2,1)S(1)}, bf16[14,128,128]{2,1,0:T(8,128)(2,1)S(1)}, u32[]{:S(2)}, u32[]{:S(2)}) %collective-permute-start.5) | collective-permute-done | bytes 458784 | tf_op jit(solution)/shard_map/ppermute | solution.py:12
  47.0 1.4 %gather_fusion.15 = bf16[14,128,128]{2,1,0:T(8,128)(2,1)} fusion(bf16[14,128,128]{2,1,0:T(8,128)(2,1)S(1)} %collective-permute-done.5, s32[1024]{0:T(1024)S(1)} %pad_clamp_fusion), kind=kCustom, calls=%fused_computation.15.clone | custom fusion | bytes 917560 | tf_op jit(solution)/shard_map/jit(_take)/gather | solution.py:22
  48.4 0.6 gather_fusion.13
  49.1 53.4 %all-reduce.4.cloned.1.call-done = (bf16[14,128,128]{2,1,0:T(8,128)(2,1)}, bf16[14,128,128]{2,1,0:T(8,128)(2,1)}, bf16[14,128,128]{2,1,0:T(8,128)(2,1)}, bf16[14...) async-done(((bf16[14,128,128]{2,1,0:T(8,128)(2,1)}, ...) | async-done | bytes 3670032 | tf_op jit(solution)/shard_map/psum | solution.py:17
  102.5 1.6 %fusion = f32[14,128,128]{2,1,0:T(8,128)S(1)} fusion(bf16[14,128,128]{2,1,0:T(8,128)(2,1)} %get-tuple-element.15, bf16[14,128,128]{2,1,0:T(8,128)(2,1)} %gather_fusion.15, pred[14]{0:T(512)(128)(4,1)S(1)} %get-tuple-element.37), kind=kOutput, calls=%fused_computation.17 | convolution fusion | flops 58949632 | bytes 1835022 | tf_op jit(solution)/shard_map/mab,mbc->mac/dot_general | solution.py:24
  104.1 0.0 copy-done.9
  104.1 0.0 copy-start.2
  104.1 0.0 copy-start.8
  104.1 0.4 fusion.2
  104.5 0.6 copy-done.2
  105.1 0.1 copy-done.8
  105.2 0.4 fusion.4
  105.6 0.7 copy-done.7
  106.3 0.4 fusion.6
  106.6 0.7 copy-done.6
  107.3 0.4 fusion.8
  107.6 0.7 copy-done.5
  108.3 0.4 fusion.10
  108.7 0.6 copy-done.4
  109.3 0.4 fusion.12
  109.7 0.6 copy-done.3
  110.3 0.4 fusion.14
  110.7 2.3 %add_convert_fusion = bf16[14,2,128,128]{3,2,1,0:T(8,128)(2,1)} fusion(f32[14,128,128]{2,1,0:T(8,128)S(1)} %fusion, f32[14,2]{1,0:T(8,128)S(1)} %copy.19, f32[14,128,128]{2,1,0:T(8,128)S(1)} %fusion.2, f32[14,2]{1,0:T(8,128)S(1)} %copy.18, f32[14,128,128]{2,1,0:T(8,128)S(1)} %fusion.4, f32[14,2]{1,0:T(8,128)S(1)} %copy.17, f32[14,128,128]{2,1,0:T(8,128)S(1)} %fusion.6, ...), kind=kLoop, calls=%fused_computation.16 | loop fusion | flops 7340032 | bytes 8258432 | tf_op jit(solution)/shard_map/convert_element_type | solution.py:60
  (34 shorter events, 0.2 us)
Async XLA Ops:
  6.5 96.0 %all-reduce.4.cloned.1.call-start = ((), (), s32[]{:S(2)}) async-start(), calls=%async_computation | async-start | bytes 7340032 | tf_op jit(solution)/shard_map/psum | solution.py:17
  6.5 20.9 %collective-permute-start.1 = (bf16[14,128,128]{2,1,0:T(8,128)(2,1)}, bf16[14,128,128]{2,1,0:T(8,128)(2,1)S(1)}, u32[]{:S(2)}, u32[]{:S(2)}) collective-permute-start(bf16[14,128,128]{2,1,0:T(8,128)(2,1)} %bitcast.29), channel_id=1, source_target_pairs={{0,24},{8,0},{16,8},{24,16},{1,25},{9,1},{17,9},{25,17},{2,26},{10... | collective-permute-start | bytes 1376264 | tf_op jit(solution)/shard_map/ppermute | solution.py:12
  9.5 15.4 %collective-permute-start = (s32[14]{0:T(128)}, s32[14]{0:T(128)S(1)}, u32[]{:S(2)}, u32[]{:S(2)}) collective-permute-start(s32[14]{0:T(128)} %bitcast.26), channel_id=1, source_target_pairs={{0,24},{8,0},{16,8},{24,16},{1,25},{9,1},{17,9},{25,17},{2,26},{10... | collective-permute-start | bytes 176 | tf_op jit(solution)/shard_map/ppermute | solution.py:12
  12.7 0.7 copy-start
  13.3 9.6 %copy-start.1 = (bf16[14,1,128,128]{3,2,1,0:T(8,128)(2,1)S(1)}, bf16[14,1,128,128]{3,2,1,0:T(8,128)(2,1)}, u32[]{:S(2)}) copy-start(bf16[14,1,128,128]{3,2,1,0:T(8,128)(2,1)} %param.7) | copy-start | bytes 1376260
  25.0 2.8 %collective-permute-start.2 = (s32[14]{0:T(128)S(1)}, s32[14]{0:T(128)S(1)}, u32[]{:S(2)}, u32[]{:S(2)}) collective-permute-start(s32[14]{0:T(128)S(1)} %collective-permute-done), channel_id=1, source_target_pairs={{0,24},{8,0},{16,8},{24,16},{1,25},{9,1},{17,9},{25,17},{2,26},{10... | collective-permute-start | bytes 176 | tf_op jit(solution)/shard_map/ppermute | solution.py:12
  27.5 10.6 %collective-permute-start.3 = (bf16[14,128,128]{2,1,0:T(8,128)(2,1)S(1)}, bf16[14,128,128]{2,1,0:T(8,128)(2,1)S(1)}, u32[]{:S(2)}, u32[]{:S(2)}) collective-permute-start(bf16[14,128,128]{2,1,0:T(8,128)(2,1)S(1)} %collective-permute-done.1), channel_id=1, source_target_pairs={{0,24},{8,0},{16,8},{24,16},{1,25},{9,1},{17,9},{25,17},{2,26},{10... | collective-permute-start | bytes 1376264 | tf_op jit(solution)/shard_map/ppermute | solution.py:12
  27.8 9.6 %collective-permute-start.4 = (s32[14]{0:T(128)S(1)}, s32[14]{0:T(128)S(1)}, u32[]{:S(2)}, u32[]{:S(2)}) collective-permute-start(s32[14]{0:T(128)S(1)} %collective-permute-done.2), channel_id=1, source_target_pairs={{0,24},{8,0},{16,8},{24,16},{1,25},{9,1},{17,9},{25,17},{2,26},{10... | collective-permute-start | bytes 176 | tf_op jit(solution)/shard_map/ppermute | solution.py:12
  30.6 9.1 %copy-start.10 = (s32[14,2]{0,1:T(2,128)S(1)}, s32[14,2]{0,1:T(2,128)}, u32[]{:S(2)}) copy-start(s32[14,2]{0,1:T(2,128)} %param.9) | copy-start | bytes 340
  38.0 9.0 %collective-permute-start.5 = (bf16[14,128,128]{2,1,0:T(8,128)(2,1)S(1)}, bf16[14,128,128]{2,1,0:T(8,128)(2,1)S(1)}, u32[]{:S(2)}, u32[]{:S(2)}) collective-permute-start(bf16[14,128,128]{2,1,0:T(8,128)(2,1)S(1)} %collective-permute-done.3), channel_id=1, source_target_pairs={{0,24},{8,0},{16,8},{24,16},{1,25},{9,1},{17,9},{25,17},{2,26},{10... | collective-permute-start | bytes 1376264 | tf_op jit(solution)/shard_map/ppermute | solution.py:12
  102.5 1.6 %copy-start.9 = (bf16[14,128,128]{2,1,0:T(8,128)(2,1)S(1)}, bf16[14,128,128]{2,1,0:T(8,128)(2,1)}, u32[]{:S(2)}) copy-start(bf16[14,128,128]{2,1,0:T(8,128)(2,1)} %get-tuple-element.16) | copy-start | bytes 1376260
  104.1 1.0 copy-start.2
  104.1 1.1 copy-start.8
  105.2 1.0 copy-start.7
  106.3 1.0 copy-start.6
  107.3 1.0 copy-start.5
  108.3 1.0 copy-start.4
  109.3 1.0 copy-start.3
Sparse Core Ops, SparseCore 0:
  12.8 89.6 all-reduce.3
where the time goes:
time: 121 us; the launch traced here: 120 us
  waiting for transfers between devices  62.8 us (52%)
  local copies, waits for them, and re-layouts  17.3 us (14%)
  between operations  13.7 us (11%)
  blocking collectives  8.74 us (7%)
  starting transfers between devices  7.87 us (7%)
  other arithmetic  5.35 us (4%)
  matrix products  4.07 us (3%)
    psum x1, waiting for transfers between devices, broadcast(): return lax.psum(kept, axis)  53.4 us
    ppermute x6, waiting for transfers between devices, passed_along(): return lax.ppermute(value, axis, pairs)  9.34 us
    psum x1, blocking collectives, broadcast(): return lax.psum(kept, axis)  8.74 us
    ppermute x6, starting transfers between devices, passed_along(): return lax.ppermute(value, axis, pairs)  7.87 us
    gather x8, local copies, waits for them, and re-layouts, add_products(): chosen = jnp.take(b_blocks, index, axis=0)  6.57 us
    gather x8, local copies, waits for them, and re-layouts, add_products(): landing = jnp.take(b_cols, index, axis=0)  5.26 us
    unnamed x22, local copies, waits for them, and re-layouts  4.68 us
    dot_general x8, matrix products, add_products(): jnp.einsum('mab,mbc->mac', a_blocks, chosen, preferred_element_type=jnp.f...  4.07 us
  transfers between devices with their start and end apart: 7, of which 4 were waited for; matrix products, arithmetic and copies ran while one was open for 13% of the time, Pallas kernels for 0%

commit v1 on v0

--- a/solution.py
+++ b/solution.py
@@ -1,9 +1,15 @@
+import functools
+
 import jax
 import jax.numpy as jnp
 from jax import lax
+from jax.experimental import pallas as pl
+from jax.experimental.pallas import tpu as pltpu
 from jax.sharding import PartitionSpec as P
 
 STEPS = 4
+CORES = 2
+MESH = pl.DeviceIdType.MESH
 
 
 def passed_along(value, axis, steps):
@@ -26,7 +32,7 @@
     return total + weight[:, :, None, None] * product[:, None]
 
 
-def on_device(xblocks, xcols, outcols):
+def on_any_mesh(xblocks, xcols, outcols):
     row_count = lax.axis_size("row")
     col_count = lax.axis_size("col")
     per_panel = col_count // row_count
@@ -60,9 +66,286 @@
     return total.astype(jnp.bfloat16)
 
 
+def remote(src, dst, send_sem, recv_sem, row, col):
+    return pltpu.make_async_remote_copy(
+        src_ref=src,
+        dst_ref=dst,
+        send_sem=send_sem,
+        recv_sem=recv_sem,
+        device_id=(row, col),
+        device_id_type=MESH,
+    )
+
+
+def kernel(
+    xc_ref, oc_ref, x_ref, o_ref,
+    a_buf, b_buf, acc, meta_v, meta_s,
+    meta_send, meta_recv, meta_loc, own_loc,
+    right_send, left_send, lane_recv, sib_send, sib_recv,
+    row_send, row_fwd, row_recv,
+):
+    rows = x_ref.shape[0]
+    half = rows // 2
+    chips = STEPS
+    i = lax.axis_index("row")
+    j = lax.axis_index("col")
+    z, c = j // CORES, j % CORES
+    y, x = i // 2, i % 2
+    xn = 2 * y + (1 - x)
+    yn = 2 * (1 - y) + x
+    dg = 2 * (1 - y) + (1 - x)
+    row_peers = (xn, yn, dg)
+    col_peers = [lax.rem(j + d, CORES * chips) for d in range(1, CORES * chips)]
+
+    barrier = pltpu.get_barrier_semaphore()
+    for r in row_peers:
+        pl.semaphore_signal(barrier, inc=1, device_id=(r, j), device_id_type=MESH)
+    for q in col_peers:
+        pl.semaphore_signal(barrier, inc=1, device_id=(i, q), device_id_type=MESH)
+
+    lane = lax.broadcasted_iota(jnp.int32, (8, 128), 1)
+    vec = jnp.zeros((8, 128), jnp.int32)
+    for m in range(rows):
+        vec = jnp.where(lane == m, xc_ref[m, 0], vec)
+    meta_v[j] = vec
+    meta_v[CORES * chips + i] = vec
+    own = pltpu.make_async_copy(x_ref.at[:, 0], a_buf.at[j], own_loc.at[0])
+    own_b = pltpu.make_async_copy(x_ref.at[:, 0], b_buf.at[i], own_loc.at[1])
+    own.start()
+    own_b.start()
+    pl.semaphore_wait(barrier, len(row_peers) + len(col_peers))
+
+    metas = []
+    slot = CORES * chips + i
+    for n, r in enumerate(row_peers):
+        metas.append(
+            (remote(meta_v.at[slot], meta_v.at[slot], meta_send.at[n], meta_recv.at[slot], r, j), CORES * chips + r)
+        )
+    for n, q in enumerate(col_peers):
+        metas.append((remote(meta_v.at[j], meta_v.at[j], meta_send.at[3 + n], meta_recv.at[j], i, q), q))
+    for copy, _ in metas:
+        copy.start()
+
+    def part(k):
+        return pl.ds(k * half, half)
+
+    def own_part(k):
+        return x_ref.at[part(k), 0]
+
+    def a_part(zs, core, k):
+        return a_buf.at[CORES * zs + core, part(k)]
+
+    def src_of(d, zs, k):
+        return own_part(k) if d == 0 else a_part(zs, c, k)
+
+    def to_right(d, zs, k):
+        return remote(
+            src_of(d, zs, k), a_part(zs, c, k), right_send.at[d, k], lane_recv.at[zs, k], i, j + CORES
+        )
+
+    def to_left(d, zs, k):
+        return remote(
+            src_of(d, zs, k), a_part(zs, c, k), left_send.at[d, k], lane_recv.at[zs, k], i, j - CORES
+        )
+
+    def to_sib(d, zs, k):
+        return remote(
+            src_of(d, zs, k), a_part(zs, c, k), sib_send.at[zs, k], sib_recv.at[zs, k], i, j + 1 - 2 * c
+        )
+
+    def lane_wait(zs, k):
+        remote(a_part(zs, c, k), a_part(zs, c, k), sib_send.at[zs, k], lane_recv.at[zs, k], i, j + 1 - 2 * c).wait_recv()
+
+    def sib_wait(zs, k):
+        there = a_part(zs, 1 - c, k)
+        remote(there, there, sib_send.at[zs, k], sib_recv.at[zs, k], i, j + 1 - 2 * c).wait_recv()
+
+    def b_part(p, k):
+        return b_buf.at[p, part(k)]
+
+    def row_copy(n, k):
+        return remote(own_part(k), b_part(i, k), row_send.at[n, k], row_recv.at[i, k], row_peers[n], j)
+
+    def row_wait(p, k):
+        remote(b_part(p, k), b_part(p, k), row_fwd.at[0], row_recv.at[p, k], xn, j).wait_recv()
+
+    fwd_y = remote(b_part(xn, 0), b_part(xn, 0), row_fwd.at[0], row_recv.at[xn, 0], yn, j)
+    fwd_x = remote(b_part(yn, 1), b_part(yn, 1), row_fwd.at[1], row_recv.at[yn, 1], xn, j)
+
+    inner_right = z < chips - 1
+    inner_left = z > 0
+    for k in range(2):
+        pl.when(inner_right)(lambda k=k: to_right(0, z, k).start())
+        pl.when(inner_left)(lambda k=k: to_left(0, z, k).start())
+        row_copy(0, k).start()
+        row_copy(1, 1 - k).start()
+    for k in range(2):
+        to_sib(0, z, k).start()
+
+    for d in (1, 2, 3):
+        for k in range(2):
+            def from_left(d=d, k=k):
+                lane_wait(z - d, k)
+                pl.when(inner_right)(lambda: to_right(d, z - d, k).start())
+                to_sib(d, z - d, k).start()
+
+            def from_right(d=d, k=k):
+                lane_wait(z + d, k)
+                pl.when(inner_left)(lambda: to_left(d, z + d, k).start())
+                to_sib(d, z + d, k).start()
+
+            if d < 3:
+                pl.when(z - d >= 0)(from_left)
+                pl.when(z + d <= chips - 1)(from_right)
+            if d == 1 and k == 0:
+                row_wait(xn, 0)
+                fwd_y.start()
+                row_wait(yn, 1)
+                fwd_x.start()
+                for copy, source in metas:
+                    there = meta_v.at[source]
+                    remote(there, there, meta_send.at[0], meta_recv.at[source], xn, j).wait_recv()
+                for copy, _ in metas:
+                    copy.wait_send()
+                down = pltpu.make_async_copy(meta_v, meta_s, meta_loc)
+                down.start()
+                down.wait()
+
+    row_wait(xn, 1)
+    row_wait(yn, 0)
+    row_wait(dg, 0)
+    row_wait(dg, 1)
+    own.wait()
+    own_b.wait()
+
+    first = z // 2
+    last = (chips - 1) * (1 - first)
+
+    def operands(m, zs):
+        left, right = [], []
+        for h in range(CORES):
+            t = CORES * zs + h
+            at = h * half + meta_s[t, 0, m]
+            block = b_buf[zs, at]
+            landing = meta_s[CORES * chips + zs, 0, at]
+            zero = jnp.zeros_like(block)
+            right.append(
+                jnp.concatenate(
+                    [jnp.where(landing == oc_ref[m, o], block, zero) for o in range(2)], axis=1
+                )
+            )
+            left.append(a_buf[t, m])
+        return left, right
+
+    def product(m, sources):
+        left, right = [], []
+        for zs in sources:
+            more = operands(m, zs)
+            left += more[0]
+            right += more[1]
+        return jnp.dot(
+            jnp.concatenate(left, axis=1), jnp.concatenate(right, axis=0), preferred_element_type=jnp.float32
+        )
+
+    def near(n):
+        return n + first
+
+    def wait_sib_near(k):
+        for n in range(chips - 1):
+            sib_wait(near(n), k)
+
+    far = last
+
+    def far_lane(k):
+        def from_left():
+            lane_wait(0, k)
+            to_sib(3, far, k).start()
+
+        def from_right():
+            lane_wait(chips - 1, k)
+            to_sib(3, far, k).start()
+
+        pl.when(z == chips - 1)(from_left)
+        pl.when(z == 0)(from_right)
+
+    def early(m, carry):
+        acc[m] = product(m, [near(n) for n in range(chips - 1)])
+        return carry
+
+    def late(m, carry):
+        total = acc[m] + product(m, [far])
+        for o in range(2):
+            o_ref[m, o] = total[:, o * 128 : (o + 1) * 128].astype(o_ref.dtype)
+        return carry
+
+    for k in range(2):
+        wait_sib_near(k)
+        lax.fori_loop(k * half, (k + 1) * half, early, 0)
+    for k in range(2):
+        far_lane(k)
+        sib_wait(far, k)
+        lax.fori_loop(k * half, (k + 1) * half, late, 0)
+
+    for k in range(2):
+        for n in range(2):
+            row_copy(n, k).wait_send()
+        for d in range(chips):
+            def right_done(d=d, k=k):
+                to_right(d, z - d, k).wait_send()
+
+            def left_done(d=d, k=k):
+                to_left(d, z + d, k).wait_send()
+
+            if d < chips - 1:
+                pl.when(jnp.logical_and(inner_right, z - d >= 0))(right_done)
+                pl.when(jnp.logical_and(inner_left, z + d <= chips - 1))(left_done)
+            to_sib(1, d, k).wait_send()
+    fwd_y.wait_send()
+    fwd_x.wait_send()
+
+
+def on_four_by_eight(xblocks, xcols, outcols):
+    rows, _, size, _ = xblocks.shape
+    kept = outcols.shape[1]
+    slots = CORES * STEPS + STEPS
+    dma = pltpu.SemaphoreType.DMA
+    return pl.pallas_call(
+        kernel,
+        out_shape=jax.ShapeDtypeStruct((rows, kept, size, size), jnp.bfloat16),
+        in_specs=[
+            pl.BlockSpec(memory_space=pltpu.SMEM),
+            pl.BlockSpec(memory_space=pltpu.SMEM),
+            pl.BlockSpec(memory_space=pltpu.VMEM),
+        ],
+        out_specs=pl.BlockSpec(memory_space=pltpu.VMEM),
+        scratch_shapes=[
+            pltpu.VMEM((CORES * STEPS, rows, size, size), jnp.bfloat16),
+            pltpu.VMEM((STEPS, rows, size, size), jnp.bfloat16),
+            pltpu.VMEM((rows, size, kept * size), jnp.float32),
+            pltpu.VMEM((slots, 8, 128), jnp.int32),
+            pltpu.SMEM((slots, 8, 128), jnp.int32),
+            dma((10,)),
+            dma((slots,)),
+            dma,
+            dma((2,)),
+            dma((STEPS, 2)),
+            dma((STEPS, 2)),
+            dma((STEPS, 2)),
+            dma((STEPS, 2)),
+            dma((STEPS, 2)),
+            dma((2, 2)),
+            dma((2,)),
+            dma((STEPS, 2)),
+        ],
+        compiler_params=pltpu.CompilerParams(
+            collective_id=0, has_side_effects=True, vmem_limit_bytes=32 * 1024 * 1024
+        ),
+    )(xcols, outcols, xblocks)
+
+
 def solution(mesh):
     in_specs = (P("row", "col", None, None), P("row", "col"), P("row", "col"))
     out_specs = P("row", "col", None, None)
-    return jax.shard_map(
-        on_device, mesh=mesh, in_specs=in_specs, out_specs=out_specs, check_vma=False
-    )
+    fits = mesh.shape["row"] == STEPS and mesh.shape["col"] == CORES * STEPS
+    body = on_four_by_eight if fits else on_any_mesh
+    return jax.shard_map(body, mesh=mesh, in_specs=in_specs, out_specs=out_specs, check_vma=False)

time: 121 us -> 43.5 us (0.36)
  waiting for transfers between devices: 62.8 us -> 0 us
  Pallas kernels: 0 us -> 40.5 us
  local copies, waits for them, and re-layouts: 17.3 us -> 2.8 us
  between operations: 13.7 us -> 0.01 us
  blocking collectives: 8.74 us -> 0 us
  starting transfers between devices: 7.87 us -> 0 us
  other arithmetic: 5.35 us -> 0 us
  matrix products: 4.07 us -> 0 us
    psum x1 -> x0, waiting for transfers between devices: 53.4 us -> none  [broadcast(): return lax.psum(kept, axis)]
    pallas_call x0 -> x1, Pallas kernels: none -> 40.5 us  [on_four_by_eight(): pl.pallas_call(kernel, out_shape=jax.ShapeDtypeStruct((rows, kept, size,...]
    gather x16 -> x0, local copies, waits for them, and re-layouts: 11.8 us -> none  [the longest x8 6.57 us: add_products(): chosen = jnp.take(b_blocks, index, axis=0)]
    ppermute x6 -> x0, waiting for transfers between devices: 9.34 us -> none  [passed_along(): return lax.ppermute(value, axis, pairs)]
    psum x1 -> x0, blocking collectives: 8.74 us -> none  [broadcast(): return lax.psum(kept, axis)]
    ppermute x6 -> x0, starting transfers between devices: 7.87 us -> none  [passed_along(): return lax.ppermute(value, axis, pairs)]
    dot_general x8 -> x0, matrix products: 4.07 us -> none  [add_products(): jnp.einsum('mab,mbc->mac', a_blocks, chosen, preferred_element_type=jnp.f...]
    select_n x14 -> x0, other arithmetic: 2.98 us -> none  [the longest x2 2.9 us: broadcast(): jnp.where(lax.axis_index(axis) == source, value, 0).astype(value.dtype)]
  transfers between devices with their start and end apart: 7 -> 0, of which waited for: 4 -> 0; matrix products, arithmetic and copies ran while one was open for 13% -> 0% of each run, Pallas kernels for 0% -> 0%
where the time goes in v1:
time: 43.5 us; the launch traced here: 43.3 us
  Pallas kernels  40.5 us (93%)
  local copies, waits for them, and re-layouts  2.8 us (6%)
    pallas_call x1, Pallas kernels, on_four_by_eight(): pl.pallas_call(kernel, out_shape=jax.ShapeDtypeStruct((rows, kept, size,...  40.5 us
    unnamed x7, local copies, waits for them, and re-layouts  2.8 us

profile of v1, /device:TPU:1, one launch (start us, length us, event | category | flops | bytes accessed | tf_op | source)
XLA Modules:
  0.0 43.3 jit_solution(13515970280777675615)
XLA Ops:
  0.0 0.0 copy-start.1
  0.0 0.8 %copy.4.xc_ref = s32[14,1]{1,0:T(8,128)S(1)} copy(s32[14,1]{0,1:T(1,128)} %param.4) | data formatting | bytes 112 | tf_op args[1]
  0.8 0.0 copy-done.1
  0.8 0.1 copy.5.oc_ref
  0.9 0.0 copy-start
  0.9 1.0 %copy-done = bf16[14,1,128,128]{3,2,1,0:T(8,128)(2,1)S(1)} copy-done((bf16[14,1,128,128]{3,2,1,0:T(8,128)(2,1)S(1)}, bf16[14,1,128,128]{3,2,1,0:T(8,128)(2,1)}, u32[]{:S(2)}) %copy-start) | copy-done | bytes 458776
  1.9 40.5 %shard_map.37 = bf16[14,2,128,128]{3,2,1,0:T(8,128)(2,1)S(1)} custom-call(s32[14,1]{1,0:T(8,128)S(1)} %copy.4.xc_ref, s32[14,2]{1,0:T(8,128)S(1)} %copy.5.oc_ref, bf16[14,1,128,128]{3,2,1,0:T(8,128)(2,1)S(1)} %copy-done), custom_call_target="tpu_custom_call" | custom-call | tf_op jit(solution)/shard_map/pallas_call | solution.py:312
  42.4 0.9 %copy.7 = bf16[14,2,128,128]{3,2,1,0:T(8,128)(2,1)} copy(bf16[14,2,128,128]{3,2,1,0:T(8,128)(2,1)S(1)} %shard_map.37) | data formatting | bytes 1835008
Async XLA Ops:
  0.0 0.8 %copy-start.1 = (s32[14,2]{0,1:T(2,128)S(1)}, s32[14,2]{0,1:T(2,128)}, u32[]{:S(2)}) copy-start(s32[14,2]{0,1:T(2,128)} %param.5) | copy-start | bytes 340
  0.9 1.0 %copy-start = (bf16[14,1,128,128]{3,2,1,0:T(8,128)(2,1)S(1)}, bf16[14,1,128,128]{3,2,1,0:T(8,128)(2,1)}, u32[]{:S(2)}) copy-start(bf16[14,1,128,128]{3,2,1,0:T(8,128)(2,1)} %x_ref.1) | copy-start | bytes 1376260

commit v2 on v0

--- a/solution.py
+++ b/solution.py
@@ -1,9 +1,16 @@
+import functools
+
 import jax
 import jax.numpy as jnp
 from jax import lax
+from jax.experimental import pallas as pl
+from jax.experimental.pallas import tpu as pltpu
 from jax.sharding import PartitionSpec as P
 
 STEPS = 4
+CORES = 2
+PIECE = 2
+MESH = pl.DeviceIdType.MESH
 
 
 def passed_along(value, axis, steps):
@@ -26,7 +33,7 @@
     return total + weight[:, :, None, None] * product[:, None]
 
 
-def on_device(xblocks, xcols, outcols):
+def on_any_mesh(xblocks, xcols, outcols):
     row_count = lax.axis_size("row")
     col_count = lax.axis_size("col")
     per_panel = col_count // row_count
@@ -60,9 +67,294 @@
     return total.astype(jnp.bfloat16)
 
 
+def remote(src, dst, send_sem, recv_sem, row, col):
+    return pltpu.make_async_remote_copy(
+        src_ref=src,
+        dst_ref=dst,
+        send_sem=send_sem,
+        recv_sem=recv_sem,
+        device_id=(row, col),
+        device_id_type=MESH,
+    )
+
+
+def kernel(
+    xc_ref, oc_ref, x_ref, o_ref,
+    a_buf, b_buf, acc, meta_v, meta_s, oc_s,
+    meta_loc, own_loc,
+    right_send, left_send, lane_recv, sib_send, sib_recv,
+    row_send, row_fwd, row_recv,
+):
+    rows = x_ref.shape[0]
+    half = rows // 2
+    chips = STEPS
+    pieces = rows // PIECE
+    meta = pieces
+    i = lax.axis_index("row")
+    j = lax.axis_index("col")
+    z, c = j // CORES, j % CORES
+    y, x = i // 2, i % 2
+    xn = 2 * y + (1 - x)
+    yn = 2 * (1 - y) + x
+    dg = 2 * (1 - y) + (1 - x)
+    sib = j + 1 - 2 * c
+    right, left = j + CORES, j - CORES
+    inner_right = z < chips - 1
+    inner_left = z > 0
+    tiles = CORES * chips
+
+    barrier = pltpu.get_barrier_semaphore()
+
+    def greet(row, col):
+        pl.semaphore_signal(barrier, inc=1, device_id=(row, col), device_id_type=MESH)
+
+    greet(i, sib)
+    pl.when(inner_right)(lambda: greet(i, right))
+    pl.when(inner_left)(lambda: greet(i, left))
+    greet(xn, j)
+    greet(yn, j)
+
+    own = pltpu.make_async_copy(x_ref.at[:, 0], a_buf.at[j], own_loc.at[0])
+    own_b = pltpu.make_async_copy(x_ref.at[:, 0], b_buf.at[i], own_loc.at[1])
+    own.start()
+    own_b.start()
+    oc_down = pltpu.make_async_copy(oc_ref, oc_s, own_loc.at[2])
+    oc_down.start()
+    meta_v[j, 0:1, 0:rows] = xc_ref[...]
+    meta_v[tiles + i, 0:1, 0:rows] = xc_ref[...]
+    pl.semaphore_wait(barrier, 5 - jnp.where(jnp.logical_and(inner_left, inner_right), 0, 1))
+
+    def part(k):
+        return pl.ds(k * PIECE, PIECE)
+
+    def there(zs, core, k):
+        if k is meta:
+            return meta_v.at[CORES * zs + core]
+        return a_buf.at[CORES * zs + core, part(k)]
+
+    def here(d, zs, k):
+        if k is meta or d != 0:
+            return there(zs, c, k)
+        return x_ref.at[part(k), 0]
+
+    def to_right(d, zs, k):
+        return remote(here(d, zs, k), there(zs, c, k), right_send.at[d, k], lane_recv.at[zs, k], i, right)
+
+    def to_left(d, zs, k):
+        return remote(here(d, zs, k), there(zs, c, k), left_send.at[d, k], lane_recv.at[zs, k], i, left)
+
+    def to_sib(d, zs, k):
+        return remote(here(d, zs, k), there(zs, c, k), sib_send.at[zs, k], sib_recv.at[zs, k], i, sib)
+
+    def lane_wait(zs, k):
+        remote(there(zs, c, k), there(zs, c, k), sib_send.at[zs, k], lane_recv.at[zs, k], i, sib).wait_recv()
+
+    def sib_wait(zs, k):
+        mine = there(zs, 1 - c, k)
+        remote(mine, mine, sib_send.at[zs, k], sib_recv.at[zs, k], i, sib).wait_recv()
+
+    def b_part(p, k):
+        if k == 2:
+            return meta_v.at[tiles + p]
+        return b_buf.at[p, pl.ds(k * half, half)]
+
+    def row_copy(n, k):
+        source = b_part(i, k) if k == 2 else x_ref.at[pl.ds(k * half, half), 0]
+        return remote(source, b_part(i, k), row_send.at[n, k], row_recv.at[i, k], (xn, yn)[n], j)
+
+    def row_wait(p, k):
+        remote(b_part(p, k), b_part(p, k), row_fwd.at[0], row_recv.at[p, k], xn, j).wait_recv()
+
+    def row_forward(n, k):
+        p, to = ((xn, yn), (yn, xn))[n]
+        return remote(b_part(p, k), b_part(p, k), row_fwd.at[k], row_recv.at[p, k], to, j)
+
+    forwards = [row_forward(0, 0), row_forward(1, 1), row_forward(0, 2)]
+
+    def own_out(k):
+        pl.when(inner_right)(lambda: to_right(0, z, k).start())
+        pl.when(inner_left)(lambda: to_left(0, z, k).start())
+
+    own_out(meta)
+    row_copy(0, 2).start()
+    row_copy(1, 2).start()
+    lax.fori_loop(0, pieces, lambda k, n: (own_out(k), n)[1], 0)
+    for k in range(2):
+        row_copy(0, k).start()
+        row_copy(1, 1 - k).start()
+    to_sib(0, z, meta).start()
+    lax.fori_loop(0, pieces, lambda k, n: (to_sib(0, z, k).start(), n)[1], 0)
+
+    def from_left(d, k):
+        lane_wait(z - d, k)
+        if d < chips - 1:
+            pl.when(inner_right)(lambda: to_right(d, z - d, k).start())
+        to_sib(d, z - d, k).start()
+
+    def from_right(d, k):
+        lane_wait(z + d, k)
+        if d < chips - 1:
+            pl.when(inner_left)(lambda: to_left(d, z + d, k).start())
+        to_sib(d, z + d, k).start()
+
+    def arrive(d, k):
+        pl.when(z - d >= 0)(lambda: from_left(d, k))
+        pl.when(z + d <= chips - 1)(lambda: from_right(d, k))
+
+    def arrive_loop(d):
+        arrive(d, meta)
+        lax.fori_loop(0, pieces, lambda k, n: (arrive(d, k), n)[1], 0)
+
+    arrive_loop(1)
+    row_wait(xn, 2)
+    forwards[2].start()
+    row_wait(xn, 0)
+    forwards[0].start()
+    row_wait(yn, 1)
+    forwards[1].start()
+    arrive_loop(2)
+    row_wait(yn, 2)
+    row_wait(dg, 2)
+    row_wait(xn, 1)
+    row_wait(yn, 0)
+    row_wait(dg, 0)
+    row_wait(dg, 1)
+    own.wait()
+    own_b.wait()
+    oc_down.wait()
+
+    first = z // 2
+    far = (chips - 1) * (1 - first)
+
+    def near(n):
+        return n + first
+
+    def lower(start, count):
+        down = pltpu.make_async_copy(meta_v.at[pl.ds(start, count)], meta_s.at[pl.ds(start, count)], meta_loc)
+        down.start()
+        down.wait()
+
+    for n in range(chips - 1):
+        sib_wait(near(n), meta)
+    lower(CORES * first, CORES * (chips - 1))
+    lower(tiles, chips)
+
+    def operands(m, zs):
+        lhs, rhs = [], []
+        for h in range(CORES):
+            t = CORES * zs + h
+            at = h * half + meta_s[t, 0, m]
+            block = b_buf[zs, at]
+            landing = meta_s[tiles + zs, 0, at]
+            zero = jnp.zeros_like(block)
+            rhs.append(
+                jnp.concatenate([jnp.where(landing == oc_s[o, m], block, zero) for o in range(2)], axis=1)
+            )
+            lhs.append(a_buf[t, m])
+        return lhs, rhs
+
+    def product(m, sources):
+        lhs, rhs = [], []
+        for zs in sources:
+            more = operands(m, zs)
+            lhs += more[0]
+            rhs += more[1]
+        return jnp.dot(
+            jnp.concatenate(lhs, axis=1), jnp.concatenate(rhs, axis=0), preferred_element_type=jnp.float32
+        )
+
+    def early(k, carry):
+        for n in range(chips - 1):
+            sib_wait(near(n), k)
+        for r in range(PIECE):
+            m = k * PIECE + r
+            acc[m] = product(m, [near(n) for n in range(chips - 1)])
+        return carry
+
+    lax.fori_loop(0, pieces, early, 0)
+
+    def far_arrive(k):
+        pl.when(z == chips - 1)(lambda: from_left(chips - 1, k))
+        pl.when(z == 0)(lambda: from_right(chips - 1, k))
+
+    far_arrive(meta)
+    far_arrive(0)
+    sib_wait(far, meta)
+    lower(CORES * far, CORES)
+
+    def late(k, carry):
+        pl.when(k < pieces - 1)(lambda: far_arrive(jnp.minimum(k + 1, pieces - 1)))
+        sib_wait(far, k)
+        for r in range(PIECE):
+            m = k * PIECE + r
+            total = acc[m] + product(m, [far])
+            for o in range(2):
+                o_ref[m, o] = total[:, o * 128 : (o + 1) * 128].astype(o_ref.dtype)
+        return carry
+
+    lax.fori_loop(0, pieces, late, 0)
+
+    def sent(k):
+        for d in range(chips):
+            if d < chips - 1:
+                pl.when(jnp.logical_and(inner_right, z - d >= 0))(
+                    lambda d=d: to_right(d, z - d, k).wait_send()
+                )
+                pl.when(jnp.logical_and(inner_left, z + d <= chips - 1))(
+                    lambda d=d: to_left(d, z + d, k).wait_send()
+                )
+            to_sib(1, d, k).wait_send()
+
+    sent(meta)
+    lax.fori_loop(0, pieces, lambda k, n: (sent(k), n)[1], 0)
+    for k in range(3):
+        for n in range(2):
+            row_copy(n, k).wait_send()
+        forwards[k].wait_send()
+
+
+def on_four_by_eight(xblocks, xcols, outcols):
+    rows, _, size, _ = xblocks.shape
+    kept = outcols.shape[1]
+    slots = CORES * STEPS + STEPS
+    pieces = rows // PIECE
+    dma = pltpu.SemaphoreType.DMA
+    return pl.pallas_call(
+        kernel,
+        out_shape=jax.ShapeDtypeStruct((rows, kept, size, size), jnp.bfloat16),
+        in_specs=[
+            pl.BlockSpec(memory_space=pltpu.VMEM),
+            pl.BlockSpec(memory_space=pltpu.VMEM),
+            pl.BlockSpec(memory_space=pltpu.HBM),
+        ],
+        out_specs=pl.BlockSpec(memory_space=pltpu.VMEM),
+        scratch_shapes=[
+            pltpu.VMEM((CORES * STEPS, rows, size, size), jnp.bfloat16),
+            pltpu.VMEM((STEPS, rows, size, size), jnp.bfloat16),
+            pltpu.VMEM((rows, size, kept * size), jnp.float32),
+            pltpu.VMEM((slots, 8, 128), jnp.int32),
+            pltpu.SMEM((slots, 8, 128), jnp.int32),
+            pltpu.SMEM((kept, rows), jnp.int32),
+            dma,
+            dma((3,)),
+            dma((STEPS, pieces + 1)),
+            dma((STEPS, pieces + 1)),
+            dma((STEPS, pieces + 1)),
+            dma((STEPS, pieces + 1)),
+            dma((STEPS, pieces + 1)),
+            dma((2, 3)),
+            dma((3,)),
+            dma((STEPS, 3)),
+        ],
+        compiler_params=pltpu.CompilerParams(
+            collective_id=0, has_side_effects=True, vmem_limit_bytes=32 * 1024 * 1024
+        ),
+    )(xcols.T, outcols.T, xblocks)
+
+
 def solution(mesh):
     in_specs = (P("row", "col", None, None), P("row", "col"), P("row", "col"))
     out_specs = P("row", "col", None, None)
-    return jax.shard_map(
-        on_device, mesh=mesh, in_specs=in_specs, out_specs=out_specs, check_vma=False
-    )
+    fits = mesh.shape["row"] == STEPS and mesh.shape["col"] == CORES * STEPS
+    body = on_four_by_eight if fits else on_any_mesh
+    return jax.shard_map(body, mesh=mesh, in_specs=in_specs, out_specs=out_specs, check_vma=False)

time: 121 us -> 40.4 us (0.33)
  waiting for transfers between devices: 62.8 us -> 0 us
  Pallas kernels: 0 us -> 37.5 us
  local copies, waits for them, and re-layouts: 17.3 us -> 2.62 us
  between operations: 13.7 us -> 0.01 us
  blocking collectives: 8.74 us -> 0 us
  starting transfers between devices: 7.87 us -> 0 us
  other arithmetic: 5.35 us -> 0 us
  matrix products: 4.07 us -> 0 us
    psum x1 -> x0, waiting for transfers between devices: 53.4 us -> none  [broadcast(): return lax.psum(kept, axis)]
    pallas_call x0 -> x1, Pallas kernels: none -> 37.5 us  [on_four_by_eight(): pl.pallas_call(kernel, out_shape=jax.ShapeDtypeStruct((rows, kept, size,...]
    gather x16 -> x0, local copies, waits for them, and re-layouts: 11.8 us -> none  [the longest x8 6.57 us: add_products(): chosen = jnp.take(b_blocks, index, axis=0)]
    ppermute x6 -> x0, waiting for transfers between devices: 9.34 us -> none  [passed_along(): return lax.ppermute(value, axis, pairs)]
    psum x1 -> x0, blocking collectives: 8.74 us -> none  [broadcast(): return lax.psum(kept, axis)]
    ppermute x6 -> x0, starting transfers between devices: 7.87 us -> none  [passed_along(): return lax.ppermute(value, axis, pairs)]
    dot_general x8 -> x0, matrix products: 4.07 us -> none  [add_products(): jnp.einsum('mab,mbc->mac', a_blocks, chosen, preferred_element_type=jnp.f...]
    select_n x14 -> x0, other arithmetic: 2.98 us -> none  [the longest x2 2.9 us: broadcast(): jnp.where(lax.axis_index(axis) == source, value, 0).astype(value.dtype)]
  transfers between devices with their start and end apart: 7 -> 0, of which waited for: 4 -> 0; matrix products, arithmetic and copies ran while one was open for 13% -> 0% of each run, Pallas kernels for 0% -> 0%
where the time goes in v2:
time: 40.4 us; the launch traced here: 40.2 us
  Pallas kernels  37.5 us (93%)
  local copies, waits for them, and re-layouts  2.62 us (6%)
    pallas_call x1, Pallas kernels, on_four_by_eight(): pl.pallas_call(kernel, out_shape=jax.ShapeDtypeStruct((rows, kept, size,...  37.5 us
    unnamed x7, local copies, waits for them, and re-layouts  2.62 us

profile of v2, /device:TPU:1, one launch (start us, length us, event | category | flops | bytes accessed | tf_op | source)
XLA Modules:
  0.0 40.2 jit_solution(8697404312160782212)
XLA Ops:
  0.0 0.0 copy-start.1
  0.0 0.0 copy-start.2
  0.0 0.7 %copy-done.1 = s32[14,2]{0,1:T(2,128)S(1)} copy-done((s32[14,2]{0,1:T(2,128)S(1)}, s32[14,2]{0,1:T(2,128)}, u32[]{:S(2)}) %copy-start.1) | copy-done | bytes 136
  0.7 0.0 copy-done.2
  0.7 0.0 copy-start
  0.7 1.0 %copy-done = bf16[14,1,128,128]{3,2,1,0:T(8,128)(2,1)S(1)} copy-done((bf16[14,1,128,128]{3,2,1,0:T(8,128)(2,1)S(1)}, bf16[14,1,128,128]{3,2,1,0:T(8,128)(2,1)}, u32[]{:S(2)}) %copy-start) | copy-done | bytes 458776
  1.7 37.5 %shard_map.37 = bf16[14,2,128,128]{3,2,1,0:T(8,128)(2,1)S(1)} custom-call(s32[1,14]{1,0:T(1,128)S(1)} %bitcast.3, s32[2,14]{1,0:T(2,128)S(1)} %bitcast.2, bf16[14,1,128,128]{3,2,1,0:T(8,128)(2,1)S(1)} %copy-done), custom_call_target="tpu_custom_call" | custom-call | tf_op jit(solution)/shard_map/pallas_call | solution.py:322
  39.3 0.9 %copy.5 = bf16[14,2,128,128]{3,2,1,0:T(8,128)(2,1)} copy(bf16[14,2,128,128]{3,2,1,0:T(8,128)(2,1)S(1)} %shard_map.37) | data formatting | bytes 1835008
Async XLA Ops:
  0.0 0.7 %copy-start.1 = (s32[14,2]{0,1:T(2,128)S(1)}, s32[14,2]{0,1:T(2,128)}, u32[]{:S(2)}) copy-start(s32[14,2]{0,1:T(2,128)} %param.5) | copy-start | bytes 340
  0.0 0.7 %copy-start.2 = (s32[14,1]{0,1:T(1,128)S(1)}, s32[14,1]{0,1:T(1,128)}, u32[]{:S(2)}) copy-start(s32[14,1]{0,1:T(1,128)} %param.4) | copy-start | bytes 172
  0.7 1.0 %copy-start = (bf16[14,1,128,128]{3,2,1,0:T(8,128)(2,1)S(1)}, bf16[14,1,128,128]{3,2,1,0:T(8,128)(2,1)}, u32[]{:S(2)}) copy-start(bf16[14,1,128,128]{3,2,1,0:T(8,128)(2,1)} %x_ref.1) | copy-start | bytes 1376260

commit v3 on v2

--- a/solution.py
+++ b/solution.py
@@ -82,7 +82,7 @@
     xc_ref, oc_ref, x_ref, o_ref,
     a_buf, b_buf, acc, meta_v, meta_s, oc_s,
     meta_loc, own_loc,
-    right_send, left_send, lane_recv, sib_send, sib_recv,
+    right_send, left_send, lane_recv, sib_send, sib_recv, meta_send,
     row_send, row_fwd, row_recv,
 ):
     rows = x_ref.shape[0]
@@ -138,20 +138,34 @@
         return x_ref.at[part(k), 0]
 
     def to_right(d, zs, k):
-        return remote(here(d, zs, k), there(zs, c, k), right_send.at[d, k], lane_recv.at[zs, k], i, right)
+        done = meta_send.at[0, d] if k is meta else right_send.at[d]
+        return remote(here(d, zs, k), there(zs, c, k), done, lane_recv.at[zs, k], i, right)
 
     def to_left(d, zs, k):
-        return remote(here(d, zs, k), there(zs, c, k), left_send.at[d, k], lane_recv.at[zs, k], i, left)
+        done = meta_send.at[1, d] if k is meta else left_send.at[d]
+        return remote(here(d, zs, k), there(zs, c, k), done, lane_recv.at[zs, k], i, left)
+
+    def sib_slot(d, k):
+        return k if k is meta or d == chips - 1 else 0
 
     def to_sib(d, zs, k):
-        return remote(here(d, zs, k), there(zs, c, k), sib_send.at[zs, k], sib_recv.at[zs, k], i, sib)
+        done = meta_send.at[2, zs] if k is meta else sib_send.at[zs]
+        return remote(here(d, zs, k), there(zs, c, k), done, sib_recv.at[zs, sib_slot(d, k)], i, sib)
 
     def lane_wait(zs, k):
-        remote(there(zs, c, k), there(zs, c, k), sib_send.at[zs, k], lane_recv.at[zs, k], i, sib).wait_recv()
+        remote(there(zs, c, k), there(zs, c, k), sib_send.at[zs], lane_recv.at[zs, k], i, sib).wait_recv()
 
     def sib_wait(zs, k):
         mine = there(zs, 1 - c, k)
-        remote(mine, mine, sib_send.at[zs, k], sib_recv.at[zs, k], i, sib).wait_recv()
+        remote(mine, mine, sib_send.at[zs], sib_recv.at[zs, k], i, sib).wait_recv()
+
+    def sib_wait_whole(zs):
+        mine = a_buf.at[CORES * zs + 1 - c]
+        remote(mine, mine, sib_send.at[zs], sib_recv.at[zs, 0], i, sib).wait_recv()
+
+    def sent_whole(sem):
+        whole = a_buf.at[0]
+        remote(whole, whole, sem, sib_recv.at[0, 0], i, sib).wait_send()
 
     def b_part(p, k):
         if k == 2:
@@ -183,7 +197,7 @@
         row_copy(0, k).start()
         row_copy(1, 1 - k).start()
     to_sib(0, z, meta).start()
-    lax.fori_loop(0, pieces, lambda k, n: (to_sib(0, z, k).start(), n)[1], 0)
+    remote(x_ref.at[:, 0], a_buf.at[j], sib_send.at[z], sib_recv.at[z, 0], i, sib).start()
 
     def from_left(d, k):
         lane_wait(z - d, k)
@@ -263,9 +277,10 @@
             jnp.concatenate(lhs, axis=1), jnp.concatenate(rhs, axis=0), preferred_element_type=jnp.float32
         )
 
+    for n in range(chips - 1):
+        sib_wait_whole(near(n))
+
     def early(k, carry):
-        for n in range(chips - 1):
-            sib_wait(near(n), k)
         for r in range(PIECE):
             m = k * PIECE + r
             acc[m] = product(m, [near(n) for n in range(chips - 1)])
@@ -273,18 +288,39 @@
 
     lax.fori_loop(0, pieces, early, 0)
 
+    is_end = jnp.logical_or(z == 0, z == chips - 1)
+    not_end = jnp.logical_not(is_end)
+
     def far_arrive(k):
         pl.when(z == chips - 1)(lambda: from_left(chips - 1, k))
         pl.when(z == 0)(lambda: from_right(chips - 1, k))
 
     far_arrive(meta)
     far_arrive(0)
+
+    for d in range(chips - 1):
+        go_right = jnp.logical_and(inner_right, z - d >= 0)
+        go_left = jnp.logical_and(inner_left, z + d <= chips - 1)
+        pl.when(go_right)(lambda d=d: to_right(d, z - d, meta).wait_send())
+        pl.when(go_left)(lambda d=d: to_left(d, z + d, meta).wait_send())
+        if d < chips - 2:
+            pl.when(go_right)(lambda d=d: sent_whole(right_send.at[d]))
+            pl.when(go_left)(lambda d=d: sent_whole(left_send.at[d]))
+        sent_whole(sib_send.at[near(d)])
+        to_sib(1, near(d), meta).wait_send()
+    to_sib(1, far, meta).wait_send()
+    for k in range(3):
+        for n in range(2):
+            row_copy(n, k).wait_send()
+        forwards[k].wait_send()
+
     sib_wait(far, meta)
     lower(CORES * far, CORES)
+    pl.when(not_end)(lambda: sib_wait_whole(far))
 
     def late(k, carry):
         pl.when(k < pieces - 1)(lambda: far_arrive(jnp.minimum(k + 1, pieces - 1)))
-        sib_wait(far, k)
+        pl.when(is_end)(lambda: sib_wait(far, k))
         for r in range(PIECE):
             m = k * PIECE + r
             total = acc[m] + product(m, [far])
@@ -294,23 +330,10 @@
 
     lax.fori_loop(0, pieces, late, 0)
 
-    def sent(k):
-        for d in range(chips):
-            if d < chips - 1:
-                pl.when(jnp.logical_and(inner_right, z - d >= 0))(
-                    lambda d=d: to_right(d, z - d, k).wait_send()
-                )
-                pl.when(jnp.logical_and(inner_left, z + d <= chips - 1))(
-                    lambda d=d: to_left(d, z + d, k).wait_send()
-                )
-            to_sib(1, d, k).wait_send()
-
-    sent(meta)
-    lax.fori_loop(0, pieces, lambda k, n: (sent(k), n)[1], 0)
-    for k in range(3):
-        for n in range(2):
-            row_copy(n, k).wait_send()
-        forwards[k].wait_send()
+    d = chips - 2
+    pl.when(jnp.logical_and(inner_right, z - d >= 0))(lambda: sent_whole(right_send.at[d]))
+    pl.when(jnp.logical_and(inner_left, z + d <= chips - 1))(lambda: sent_whole(left_send.at[d]))
+    sent_whole(sib_send.at[far])
 
 
 def on_four_by_eight(xblocks, xcols, outcols):
@@ -337,11 +360,12 @@
             pltpu.SMEM((kept, rows), jnp.int32),
             dma,
             dma((3,)),
+            dma((STEPS,)),
+            dma((STEPS,)),
             dma((STEPS, pieces + 1)),
+            dma((STEPS,)),
             dma((STEPS, pieces + 1)),
-            dma((STEPS, pieces + 1)),
-            dma((STEPS, pieces + 1)),
-            dma((STEPS, pieces + 1)),
+            dma((3, STEPS)),
             dma((2, 3)),
             dma((3,)),
             dma((STEPS, 3)),

time: 40.4 us -> 39.6 us (0.980)
  Pallas kernels: 37.5 us -> 36.8 us
    pallas_call x1, Pallas kernels: 37.5 us -> 36.8 us  [on_four_by_eight(): pl.pallas_call(kernel, out_shape=jax.ShapeDtypeStruct((rows, kept, size,...]
where the time goes in v3:
time: 39.6 us; the launch traced here: 39.4 us
  Pallas kernels  36.8 us (93%)
  local copies, waits for them, and re-layouts  2.62 us (7%)
    pallas_call x1, Pallas kernels, on_four_by_eight(): pl.pallas_call(kernel, out_shape=jax.ShapeDtypeStruct((rows, kept, size,...  36.8 us
    unnamed x7, local copies, waits for them, and re-layouts  2.62 us

profile of v3, /device:TPU:1, one launch (start us, length us, event | category | flops | bytes accessed | tf_op | source)
XLA Modules:
  0.0 39.4 jit_solution(3127556692759559160)
XLA Ops:
  0.0 0.0 copy-start.1
  0.0 0.0 copy-start.2
  0.0 0.7 %copy-done.1 = s32[14,2]{0,1:T(2,128)S(1)} copy-done((s32[14,2]{0,1:T(2,128)S(1)}, s32[14,2]{0,1:T(2,128)}, u32[]{:S(2)}) %copy-start.1) | copy-done | bytes 136
  0.7 0.0 copy-done.2
  0.7 0.0 copy-start
  0.7 1.0 %copy-done = bf16[14,1,128,128]{3,2,1,0:T(8,128)(2,1)S(1)} copy-done((bf16[14,1,128,128]{3,2,1,0:T(8,128)(2,1)S(1)}, bf16[14,1,128,128]{3,2,1,0:T(8,128)(2,1)}, u32[]{:S(2)}) %copy-start) | copy-done | bytes 458776
  1.7 36.8 %shard_map.37 = bf16[14,2,128,128]{3,2,1,0:T(8,128)(2,1)S(1)} custom-call(s32[1,14]{1,0:T(1,128)S(1)} %bitcast.3, s32[2,14]{1,0:T(2,128)S(1)} %bitcast.2, bf16[14,1,128,128]{3,2,1,0:T(8,128)(2,1)S(1)} %copy-done), custom_call_target="tpu_custom_call" | custom-call | tf_op jit(solution)/shard_map/pallas_call | solution.py:345
  38.5 0.9 %copy.5 = bf16[14,2,128,128]{3,2,1,0:T(8,128)(2,1)} copy(bf16[14,2,128,128]{3,2,1,0:T(8,128)(2,1)S(1)} %shard_map.37) | data formatting | bytes 1835008
Async XLA Ops:
  0.0 0.7 %copy-start.1 = (s32[14,2]{0,1:T(2,128)S(1)}, s32[14,2]{0,1:T(2,128)}, u32[]{:S(2)}) copy-start(s32[14,2]{0,1:T(2,128)} %param.5) | copy-start | bytes 340
  0.0 0.7 %copy-start.2 = (s32[14,1]{0,1:T(1,128)S(1)}, s32[14,1]{0,1:T(1,128)}, u32[]{:S(2)}) copy-start(s32[14,1]{0,1:T(1,128)} %param.4) | copy-start | bytes 172
  0.7 1.0 %copy-start = (bf16[14,1,128,128]{3,2,1,0:T(8,128)(2,1)S(1)}, bf16[14,1,128,128]{3,2,1,0:T(8,128)(2,1)}, u32[]{:S(2)}) copy-start(bf16[14,1,128,128]{3,2,1,0:T(8,128)(2,1)} %x_ref.1) | copy-start | bytes 1376260

commit v4 on v3

--- a/solution.py
+++ b/solution.py
@@ -9,7 +9,11 @@
 
 STEPS = 4
 CORES = 2
-PIECE = 2
+PIECE = 4
+
+
+def piece_sizes(rows):
+    return tuple(min(PIECE, rows - start) for start in range(0, rows, PIECE))
 MESH = pl.DeviceIdType.MESH
 
 
@@ -88,7 +92,8 @@
     rows = x_ref.shape[0]
     half = rows // 2
     chips = STEPS
-    pieces = rows // PIECE
+    sizes = piece_sizes(rows)
+    pieces = len(sizes)
     meta = pieces
     i = lax.axis_index("row")
     j = lax.axis_index("col")
@@ -125,31 +130,31 @@
     pl.semaphore_wait(barrier, 5 - jnp.where(jnp.logical_and(inner_left, inner_right), 0, 1))
 
     def part(k):
-        return pl.ds(k * PIECE, PIECE)
+        return pl.ds(sum(sizes[:k]), sizes[k])
 
     def there(zs, core, k):
-        if k is meta:
+        if k == meta:
             return meta_v.at[CORES * zs + core]
         return a_buf.at[CORES * zs + core, part(k)]
 
     def here(d, zs, k):
-        if k is meta or d != 0:
+        if k == meta or d != 0:
             return there(zs, c, k)
         return x_ref.at[part(k), 0]
 
     def to_right(d, zs, k):
-        done = meta_send.at[0, d] if k is meta else right_send.at[d]
+        done = meta_send.at[0, d] if k == meta else right_send.at[d]
         return remote(here(d, zs, k), there(zs, c, k), done, lane_recv.at[zs, k], i, right)
 
     def to_left(d, zs, k):
-        done = meta_send.at[1, d] if k is meta else left_send.at[d]
+        done = meta_send.at[1, d] if k == meta else left_send.at[d]
         return remote(here(d, zs, k), there(zs, c, k), done, lane_recv.at[zs, k], i, left)
 
     def sib_slot(d, k):
-        return k if k is meta or d == chips - 1 else 0
+        return k if k == meta or d == chips - 1 else 0
 
     def to_sib(d, zs, k):
-        done = meta_send.at[2, zs] if k is meta else sib_send.at[zs]
+        done = meta_send.at[2, zs] if k == meta else sib_send.at[zs]
         return remote(here(d, zs, k), there(zs, c, k), done, sib_recv.at[zs, sib_slot(d, k)], i, sib)
 
     def lane_wait(zs, k):
@@ -192,7 +197,8 @@
     own_out(meta)
     row_copy(0, 2).start()
     row_copy(1, 2).start()
-    lax.fori_loop(0, pieces, lambda k, n: (own_out(k), n)[1], 0)
+    for k in range(pieces):
+        own_out(k)
     for k in range(2):
         row_copy(0, k).start()
         row_copy(1, 1 - k).start()
@@ -217,7 +223,8 @@
 
     def arrive_loop(d):
         arrive(d, meta)
-        lax.fori_loop(0, pieces, lambda k, n: (arrive(d, k), n)[1], 0)
+        for k in range(pieces):
+            arrive(d, k)
 
     arrive_loop(1)
     row_wait(xn, 2)
@@ -280,13 +287,11 @@
     for n in range(chips - 1):
         sib_wait_whole(near(n))
 
-    def early(k, carry):
-        for r in range(PIECE):
-            m = k * PIECE + r
-            acc[m] = product(m, [near(n) for n in range(chips - 1)])
+    def early(m, carry):
+        acc[m] = product(m, [near(n) for n in range(chips - 1)])
         return carry
 
-    lax.fori_loop(0, pieces, early, 0)
+    lax.fori_loop(0, rows, early, 0)
 
     is_end = jnp.logical_or(z == 0, z == chips - 1)
     not_end = jnp.logical_not(is_end)
@@ -318,17 +323,18 @@
     lower(CORES * far, CORES)
     pl.when(not_end)(lambda: sib_wait_whole(far))
 
-    def late(k, carry):
-        pl.when(k < pieces - 1)(lambda: far_arrive(jnp.minimum(k + 1, pieces - 1)))
-        pl.when(is_end)(lambda: sib_wait(far, k))
-        for r in range(PIECE):
-            m = k * PIECE + r
-            total = acc[m] + product(m, [far])
-            for o in range(2):
-                o_ref[m, o] = total[:, o * 128 : (o + 1) * 128].astype(o_ref.dtype)
+    def late(m, carry):
+        total = acc[m] + product(m, [far])
+        for o in range(2):
+            o_ref[m, o] = total[:, o * 128 : (o + 1) * 128].astype(o_ref.dtype)
         return carry
 
-    lax.fori_loop(0, pieces, late, 0)
+    for k in range(pieces):
+        if k < pieces - 1:
+            far_arrive(k + 1)
+        pl.when(is_end)(lambda k=k: sib_wait(far, k))
+        start = sum(sizes[:k])
+        lax.fori_loop(start, start + sizes[k], late, 0, unroll=True)
 
     d = chips - 2
     pl.when(jnp.logical_and(inner_right, z - d >= 0))(lambda: sent_whole(right_send.at[d]))
@@ -340,7 +346,7 @@
     rows, _, size, _ = xblocks.shape
     kept = outcols.shape[1]
     slots = CORES * STEPS + STEPS
-    pieces = rows // PIECE
+    pieces = len(piece_sizes(rows))
     dma = pltpu.SemaphoreType.DMA
     return pl.pallas_call(
         kernel,

time: 39.6 us -> 39.4 us (level)
  no operation moved by 1% of the time
where the time goes in v4:
time: 39.4 us; the launch traced here: 39.2 us
  Pallas kernels  36.6 us (93%)
  local copies, waits for them, and re-layouts  2.62 us (7%)
    pallas_call x1, Pallas kernels, on_four_by_eight(): pl.pallas_call(kernel, out_shape=jax.ShapeDtypeStruct((rows, kept, size,...  36.6 us
    unnamed x7, local copies, waits for them, and re-layouts  2.62 us

profile of v4, /device:TPU:1, one launch (start us, length us, event | category | flops | bytes accessed | tf_op | source)
XLA Modules:
  0.0 39.2 jit_solution(13749599410970829559)
XLA Ops:
  0.0 0.0 copy-start.1
  0.0 0.0 copy-start.2
  0.0 0.7 %copy-done.1 = s32[14,2]{0,1:T(2,128)S(1)} copy-done((s32[14,2]{0,1:T(2,128)S(1)}, s32[14,2]{0,1:T(2,128)}, u32[]{:S(2)}) %copy-start.1) | copy-done | bytes 136
  0.7 0.0 copy-done.2
  0.7 0.0 copy-start
  0.7 1.0 %copy-done = bf16[14,1,128,128]{3,2,1,0:T(8,128)(2,1)S(1)} copy-done((bf16[14,1,128,128]{3,2,1,0:T(8,128)(2,1)S(1)}, bf16[14,1,128,128]{3,2,1,0:T(8,128)(2,1)}, u32[]{:S(2)}) %copy-start) | copy-done | bytes 458776
  1.7 36.6 %shard_map.37 = bf16[14,2,128,128]{3,2,1,0:T(8,128)(2,1)S(1)} custom-call(s32[1,14]{1,0:T(1,128)S(1)} %bitcast.3, s32[2,14]{1,0:T(2,128)S(1)} %bitcast.2, bf16[14,1,128,128]{3,2,1,0:T(8,128)(2,1)S(1)} %copy-done), custom_call_target="tpu_custom_call" | custom-call | tf_op jit(solution)/shard_map/pallas_call | solution.py:351
  38.3 0.9 %copy.5 = bf16[14,2,128,128]{3,2,1,0:T(8,128)(2,1)} copy(bf16[14,2,128,128]{3,2,1,0:T(8,128)(2,1)S(1)} %shard_map.37) | data formatting | bytes 1835008
Async XLA Ops:
  0.0 0.7 %copy-start.1 = (s32[14,2]{0,1:T(2,128)S(1)}, s32[14,2]{0,1:T(2,128)}, u32[]{:S(2)}) copy-start(s32[14,2]{0,1:T(2,128)} %param.5) | copy-start | bytes 340
  0.0 0.7 %copy-start.2 = (s32[14,1]{0,1:T(1,128)S(1)}, s32[14,1]{0,1:T(1,128)}, u32[]{:S(2)}) copy-start(s32[14,1]{0,1:T(1,128)} %param.4) | copy-start | bytes 172
  0.7 1.0 %copy-start = (bf16[14,1,128,128]{3,2,1,0:T(8,128)(2,1)S(1)}, bf16[14,1,128,128]{3,2,1,0:T(8,128)(2,1)}, u32[]{:S(2)}) copy-start(bf16[14,1,128,128]{3,2,1,0:T(8,128)(2,1)} %x_ref.1) | copy-start | bytes 1376260

commit v5 on v4

--- a/solution.py
+++ b/solution.py
@@ -113,9 +113,9 @@
     def greet(row, col):
         pl.semaphore_signal(barrier, inc=1, device_id=(row, col), device_id_type=MESH)
 
-    greet(i, sib)
     pl.when(inner_right)(lambda: greet(i, right))
     pl.when(inner_left)(lambda: greet(i, left))
+    greet(i, sib)
     greet(xn, j)
     greet(yn, j)
 
@@ -194,11 +194,12 @@
         pl.when(inner_right)(lambda: to_right(0, z, k).start())
         pl.when(inner_left)(lambda: to_left(0, z, k).start())
 
+    own_out(0)
     own_out(meta)
+    for k in range(1, pieces):
+        own_out(k)
     row_copy(0, 2).start()
     row_copy(1, 2).start()
-    for k in range(pieces):
-        own_out(k)
     for k in range(2):
         row_copy(0, k).start()
         row_copy(1, 1 - k).start()
@@ -222,8 +223,9 @@
         pl.when(z + d <= chips - 1)(lambda: from_right(d, k))
 
     def arrive_loop(d):
+        arrive(d, 0)
         arrive(d, meta)
-        for k in range(pieces):
+        for k in range(1, pieces):
             arrive(d, k)
 
     arrive_loop(1)
@@ -300,8 +302,8 @@
         pl.when(z == chips - 1)(lambda: from_left(chips - 1, k))
         pl.when(z == 0)(lambda: from_right(chips - 1, k))
 
+    far_arrive(0)
     far_arrive(meta)
-    far_arrive(0)
 
     for d in range(chips - 1):
         go_right = jnp.logical_and(inner_right, z - d >= 0)

time: 39.4 us -> 39.4 us (level)
  no operation moved by 1% of the time
where the time goes in v5:
time: 39.4 us; the launch traced here: 39.2 us
  Pallas kernels  36.6 us (93%)
  local copies, waits for them, and re-layouts  2.62 us (7%)
    pallas_call x1, Pallas kernels, on_four_by_eight(): pl.pallas_call(kernel, out_shape=jax.ShapeDtypeStruct((rows, kept, size,...  36.6 us
    unnamed x7, local copies, waits for them, and re-layouts  2.62 us

profile of v5, /device:TPU:1, one launch (start us, length us, event | category | flops | bytes accessed | tf_op | source)
XLA Modules:
  0.0 39.2 jit_solution(965751949983385204)
XLA Ops:
  0.0 0.0 copy-start.1
  0.0 0.0 copy-start.2
  0.0 0.7 %copy-done.1 = s32[14,2]{0,1:T(2,128)S(1)} copy-done((s32[14,2]{0,1:T(2,128)S(1)}, s32[14,2]{0,1:T(2,128)}, u32[]{:S(2)}) %copy-start.1) | copy-done | bytes 136
  0.7 0.0 copy-done.2
  0.7 0.0 copy-start
  0.7 1.0 %copy-done = bf16[14,1,128,128]{3,2,1,0:T(8,128)(2,1)S(1)} copy-done((bf16[14,1,128,128]{3,2,1,0:T(8,128)(2,1)S(1)}, bf16[14,1,128,128]{3,2,1,0:T(8,128)(2,1)}, u32[]{:S(2)}) %copy-start) | copy-done | bytes 458776
  1.7 36.6 %shard_map.37 = bf16[14,2,128,128]{3,2,1,0:T(8,128)(2,1)S(1)} custom-call(s32[1,14]{1,0:T(1,128)S(1)} %bitcast.3, s32[2,14]{1,0:T(2,128)S(1)} %bitcast.2, bf16[14,1,128,128]{3,2,1,0:T(8,128)(2,1)S(1)} %copy-done), custom_call_target="tpu_custom_call" | custom-call | tf_op jit(solution)/shard_map/pallas_call | solution.py:353
  38.3 0.9 %copy.5 = bf16[14,2,128,128]{3,2,1,0:T(8,128)(2,1)} copy(bf16[14,2,128,128]{3,2,1,0:T(8,128)(2,1)S(1)} %shard_map.37) | data formatting | bytes 1835008
Async XLA Ops:
  0.0 0.7 %copy-start.1 = (s32[14,2]{0,1:T(2,128)S(1)}, s32[14,2]{0,1:T(2,128)}, u32[]{:S(2)}) copy-start(s32[14,2]{0,1:T(2,128)} %param.5) | copy-start | bytes 340
  0.0 0.7 %copy-start.2 = (s32[14,1]{0,1:T(1,128)S(1)}, s32[14,1]{0,1:T(1,128)}, u32[]{:S(2)}) copy-start(s32[14,1]{0,1:T(1,128)} %param.4) | copy-start | bytes 172
  0.7 1.0 %copy-start = (bf16[14,1,128,128]{3,2,1,0:T(8,128)(2,1)S(1)}, bf16[14,1,128,128]{3,2,1,0:T(8,128)(2,1)}, u32[]{:S(2)}) copy-start(bf16[14,1,128,128]{3,2,1,0:T(8,128)(2,1)} %x_ref.1) | copy-start | bytes 1376260
